TPU v7x, 256 devices: a whole 4x4x8 slice. The times are simulated.
256 devices in a mesh: dp: 64 (over y, z_lo, x), ctx: 4 (over z_hi, core).
Axes of the slice: x: 4, y: 4, z: 8 (z_hi: 2, z_lo: 4; z = z_hi * 4 + z_lo), core: 2. Of those that a mesh axis runs over, the one named last changes fastest.
Arguments:
- hidden: bfloat16 [64, 512, 3584], P('dp', 'ctx'), may hold values from -6 to 6
- norm_gain: bfloat16 [3584], replicated, may hold values from 0.099609375 to 1.8984375
- w_query: bfloat16 [3584, 2048], P('dp'), may hold values from -0.09375 to 0.09375
- w_key: bfloat16 [3584, 512], P('dp'), may hold values from -0.09375 to 0.09375
- w_value: bfloat16 [3584, 512], P('dp'), may hold values from -0.09375 to 0.09375
- bias_query: bfloat16 [2048], replicated, may hold values from -4 to 4
- bias_key: bfloat16 [512], replicated, may hold values from -4 to 4
- bias_value: bfloat16 [512], replicated, may hold values from -4 to 4
- kv_blocks: int32 [16, 4, 4], P('ctx'), may hold values from 0 to 3, as said below
- block_counts: int32 [16, 4], P('ctx'), may hold values from 1 to 4, as said below
Outputs:
- attended: bfloat16 [64, 512, 2048], P('dp', 'ctx')
Inputs may be any that keep to these rules, and one draw needn't show every extreme that they name: Entry 0 of kv_blocks[h, b] is b itself; entries 1 to block_counts[h, b] - 1 are distinct blocks below b; later entries are valid block numbers that are not used. block_counts[h, b] is at most b + 1, and the last query block of every head has 4.
All inputs are finite; a program needn't handle non-finite values.
Results may differ from a plain program's by a relative error of at most 0.0053.
Values may be sent and summed in bfloat16 or wider, within the bound.
No kernel may reach another device: no remote copies, remote signals or barrier semaphores. Data moves between devices by JAX's collectives and lax.ppermute only.
A program may use at most 64 MiB of HBM per device.

v0:
```python
import jax
import jax.numpy as jnp
from jax import lax
from jax.sharding import PartitionSpec as P

KVH = 4
HEAD = 128
QHEADS = 16
BLOCK = 128
MAXB = 4


EPSILON = 1e-06
THETA = 1000000.0


def rms_norm(tokens, norm_gain):
    floats = tokens.astype(jnp.float32)
    meansq = jnp.mean(floats * floats, axis=-1, keepdims=True)
    return (floats * lax.rsqrt(meansq + EPSILON) * norm_gain.astype(jnp.float32)).astype(
        jnp.bfloat16
    )


def rotary(heads_in, position):
    half_size = heads_in.shape[-1] // 2
    exponent = jnp.arange(half_size, dtype=jnp.float32) * (2.0 / heads_in.shape[-1])
    inverse = jnp.power(jnp.float32(THETA), -exponent)
    angles = position[:, None] * inverse[None, :]
    cosine = jnp.cos(angles)[:, None, :]
    sine = jnp.sin(angles)[:, None, :]
    first = heads_in[..., :half_size]
    second = heads_in[..., half_size:]
    return jnp.concatenate(
        [first * cosine - second * sine, second * cosine + first * sine], axis=-1
    )


def finish_heads(summed, bias, heads, position, rotate_it):
    shaped = (summed + bias.astype(jnp.float32)).reshape(summed.shape[0], heads, HEAD)
    if rotate_it:
        shaped = rotary(shaped, position)
    return shaped.astype(jnp.bfloat16)


def fold_rows(source, pieces):
    return tuple((jnp.dot(source, piece, preferred_element_type=jnp.float32) for piece in pieces))


def sparse_head(queries, key_rows, value_rows, blocks, counts):
    nblocks = queries.shape[0] // BLOCK
    query_tiles = queries.reshape(nblocks, BLOCK, HEAD)
    key_tiles = key_rows.reshape(nblocks, BLOCK, HEAD)[blocks].reshape(nblocks, MAXB * BLOCK, HEAD)
    value_tiles = value_rows.reshape(nblocks, BLOCK, HEAD)[blocks].reshape(
        nblocks, MAXB * BLOCK, HEAD
    )
    scores = jnp.einsum(
        "qih,qjh->qij", query_tiles, key_tiles, preferred_element_type=jnp.float32
    ) * HEAD ** (-0.5)
    column = jnp.arange(MAXB * BLOCK)
    slot_of = column // BLOCK
    inside = column % BLOCK
    row_pos = jnp.arange(BLOCK)
    allowed = (slot_of[None, None, :] < counts[:, None, None]) & (
        (slot_of[None, None, :] > 0) | (inside[None, None, :] <= row_pos[None, :, None])
    )
    expo = jnp.where(allowed, jnp.exp(scores), jnp.float32(0.0))
    totals = jnp.sum(expo, axis=-1)
    probs = expo.astype(jnp.bfloat16)
    mixed = (
        jnp.einsum("qij,qjh->qih", probs, value_tiles, preferred_element_type=jnp.float32)
        / totals[..., None]
    )
    return mixed.astype(jnp.bfloat16).reshape(nblocks * BLOCK, HEAD)


def one_head(packed):
    return sparse_head(packed[0], packed[1], packed[2], packed[3], packed[4])


def body(
    hidden,
    norm_gain,
    w_query,
    w_key,
    w_value,
    bias_query,
    bias_key,
    bias_value,
    kv_blocks,
    block_counts,
):
    groups = lax.axis_size("ctx")
    device = lax.axis_index("ctx")
    tokens = hidden[0]
    local_rows = tokens.shape[0]
    seq_len = local_rows * groups
    heads_here = QHEADS // groups
    kv_here = KVH // groups
    width_query = heads_here * HEAD
    width_pair = kv_here * HEAD
    normed = rms_norm(tokens, norm_gain)
    sum_query, sum_key, sum_value = fold_rows(
        normed,
        (
            lax.all_gather(w_query, "dp", axis=0, tiled=True),
            lax.all_gather(w_key, "dp", axis=0, tiled=True),
            lax.all_gather(w_value, "dp", axis=0, tiled=True),
        ),
    )
    position = (device * local_rows + jnp.arange(local_rows, dtype=jnp.int32)).astype(jnp.float32)
    queries = finish_heads(sum_query, bias_query, QHEADS, position, True)
    key_rows = finish_heads(sum_key, bias_key, KVH, position, True)
    value_rows = finish_heads(sum_value, bias_value, KVH, position, False)
    query_send = queries.reshape(local_rows, groups, width_query)
    pair_send = jnp.concatenate([key_rows, value_rows], axis=2)
    query_got, pair_got = (
        lax.all_to_all(query_send, "ctx", split_axis=1, concat_axis=0, tiled=True),
        lax.all_to_all(pair_send, "ctx", split_axis=1, concat_axis=0, tiled=True),
    )
    queries = query_got.reshape(seq_len, heads_here, HEAD)
    key_rows = pair_got[:, 0, :width_pair].reshape(seq_len, kv_here, HEAD)
    value_rows = pair_got[:, 0, width_pair:].reshape(seq_len, kv_here, HEAD)
    group = heads_here // kv_here
    key_rows = jnp.repeat(key_rows, group, axis=1)
    value_rows = jnp.repeat(value_rows, group, axis=1)
    mixed = lax.map(
        one_head,
        (
            queries.transpose(1, 0, 2),
            key_rows.transpose(1, 0, 2),
            value_rows.transpose(1, 0, 2),
            kv_blocks,
            block_counts,
        ),
    )
    result = mixed.transpose(1, 0, 2).reshape(seq_len, 1, width_query)
    returned = lax.all_to_all(result, "ctx", split_axis=0, concat_axis=1, tiled=True)
    return returned.reshape(1, local_rows, QHEADS * HEAD)


def solution(mesh):
    placed = (
        P("dp", "ctx", None),
        P(),
        P("dp", None),
        P("dp", None),
        P("dp", None),
        P(),
        P(),
        P(),
        P("ctx", None, None),
        P("ctx", None),
    )
    return jax.shard_map(
        body, mesh=mesh, in_specs=placed, out_specs=P("dp", "ctx", None), check_vma=False
    )
```

profile of v0, /device:TPU:1, one launch (start us, length us, event | category | flops | bytes accessed | tf_op | source)
XLA Modules:
  0.0 1162.0 jit_solution(7236101994991256935)
XLA Ops:
  6.5 0.7 all-gather.8.cloned.1.call-update
  7.3 0.7 all-gather.6.cloned.1.call-update
  8.1 0.7 all-gather.4.cloned.1.call-update
  8.7 0.7 convert_element_type.56
  9.4 0.7 convert_element_type.54
  10.1 0.7 convert_element_type.60
  10.8 0.7 convert_element_type.59
  11.5 0.2 multiply_cosine_fusion
  11.9 1.5 fusion.13
  13.4 309.5 %all-gather.8.cloned.1.call-done = bf16[3584,512]{1,0:T(8,128)(2,1)} async-done(((bf16[56,512]{1,0:T(8,128)(2,1)}), bf16[3584,512]{1,0:T(8,128)(2,1)}) %all-gather.8.cloned.1.call-update) | async-done | bytes 3670032 | tf_op jit(solution)/shard_map/all_gather | solution.py:108
  322.9 3.0 fusion.17
  326.0 349.2 %all-gather.6.cloned.1.call-done = bf16[3584,512]{1,0:T(8,128)(2,1)} async-done(((bf16[56,512]{1,0:T(8,128)(2,1)}), bf16[3584,512]{1,0:T(8,128)(2,1)}) %all-gather.6.cloned.1.call-update) | async-done | bytes 3670032 | tf_op jit(solution)/shard_map/all_gather | solution.py:107
  675.1 2.8 convolution_add_fusion.2
  678.0 0.2 fusion.22
  678.3 0.9 pad_maximum_fusion.1
  679.1 47.6 %all-to-all-start.1 = ((bf16[128,4,256]{2,0,1:T(8,128)(2,1)}), bf16[128,4,256]{2,0,1:T(8,128)(2,1)S(1)}, u32[]{:S(2)}, u32[]{:S(2)}) async-start(bf16[128,4,256]{2,0,1:T(8,128)(2,1)} %pad_maximum_fusion.1), calls=%async_computation.1 | async-start | bytes 524288 | tf_op jit(solution)/shard_map/all_to_all | solution.py:119
  726.8 326.9 %all-gather.4.cloned.1.call-done = bf16[3584,2048]{1,0:T(8,128)(2,1)} async-done(((bf16[56,2048]{1,0:T(8,128)(2,1)}), bf16[3584,2048]{1,0:T(8,128)(2,1)}) %all-gather.4.cloned.1.call-update) | async-done | bytes 14680080 | tf_op jit(solution)/shard_map/all_gather | solution.py:106
  1053.6 7.3 convolution_add_fusion
  1061.0 0.3 copy.43
  1061.3 0.2 subtract_convert_fusion
  1061.5 0.8 pad_maximum_fusion
  1062.3 45.1 %all-to-all-start = ((bf16[128,4,512]{0,2,1:T(8,128)(2,1)}), bf16[128,4,512]{0,2,1:T(8,128)(2,1)S(1)}, u32[]{:S(2)}, u32[]{:S(2)}) async-start(bf16[128,4,512]{0,2,1:T(8,128)(2,1)} %bitcast.10), calls=%async_computation | async-start | bytes 1048576 | tf_op jit(solution)/shard_map/all_to_all | solution.py:118
  1107.4 11.9 %all-to-all-done = bf16[128,4,512]{0,2,1:T(8,128)(2,1)S(1)} async-done(((bf16[128,4,512]{0,2,1:T(8,128)(2,1)}), bf16[128,4,512]{0,2,1:T(8,128)(2,1)S(1)}, u32[]{:S(2)}, u32[]{:S(2)}) %all-to-all-start) | async-done | bytes 524320 | tf_op jit(solution)/shard_map/all_to_all | solution.py:118
  1119.3 0.2 copy.32
  1119.5 0.1 reshape.277
  1119.9 0.7 copy-done.1
  1120.5 15.8 %while.12 = (s32[]{:T(128)}, bf16[4,512,128]{1,2,0:T(8,128)(2,1)S(1)}, s32[4,4]{1,0:T(4,128)}, bf16[4,512,128]{2,1,0:T(8,128)(2,1)S(1)}, bf16[4,512,128]{2,1,0:T...) while((s32[]{:T(128)}, bf16[4,512,128]{1,2,0:T(8,128)(2,1)S(1)}, ...), condition=%wide.region_3.4_spmd, body=%wide.region_1.3_spmd.sunk | while | flops 135803952 | bytes 5920353 | solution.py:127
  1120.6 0.7 compare_select_fusion.2
  1121.3 0.6 gather_fusion
  1122.0 0.6 gather_fusion.1
  1122.8 0.7 fusion.45
  1123.5 0.5 fusion.46
  1124.0 0.3 fusion.47
  1124.3 0.1 copy.58
  1124.5 0.7 compare_select_fusion.2
  1125.3 0.6 gather_fusion
  1126.0 0.6 gather_fusion.1
  1126.7 0.7 fusion.45
  1127.5 0.5 fusion.46
  1128.0 0.3 fusion.47
  1128.3 0.1 copy.58
  1128.5 0.7 compare_select_fusion.2
  1129.3 0.6 gather_fusion
  1129.9 0.6 gather_fusion.1
  1130.7 0.7 fusion.45
  1131.4 0.5 fusion.46
  1132.0 0.3 fusion.47
  1132.2 0.1 copy.58
  1132.4 0.7 compare_select_fusion.2
  1133.2 0.6 gather_fusion
  1133.9 0.6 gather_fusion.1
  1134.6 0.7 fusion.45
  1135.4 0.5 fusion.46
  1135.9 0.3 fusion.47
  1136.2 0.1 copy.58
  1136.4 0.5 broadcast.299
  1136.9 1.0 reduce
  1137.9 0.2 copy.56
  1138.1 0.4 reshape.302
  1138.5 15.0 %all_to_all.48 = bf16[4,2,32768]{2,1,0:T(2,128)(2,1)S(1)} all-to-all(bf16[4,2,32768]{2,1,0:T(2,128)(2,1)S(1)} %reshape.302), channel_id=1, replica_groups=mesh['dp'=64,'ctx'=4] {'ctx'}, dimensions={0} | all-to-all | bytes 1048576 | tf_op jit(solution)/shard_map/all_to_all | solution.py:138
  1153.5 0.5 reshape.303
  1154.0 0.1 copy.46
  1154.2 0.3 copy.41
  1154.4 1.0 copy.42
  (56 shorter events, 1.9 us)
Async XLA Ops:
  6.5 316.4 %all-gather.8.cloned.1.call-start = ((), (), s32[]{:S(2)}) async-start(), calls=%async_computation.5 | async-start | bytes 3727360 | tf_op jit(solution)/shard_map/all_gather | solution.py:108
  7.3 667.9 %all-gather.6.cloned.1.call-start = ((), (), s32[]{:S(2)}) async-start(), calls=%async_computation.4 | async-start | bytes 3727360 | tf_op jit(solution)/shard_map/all_gather | solution.py:107
  8.0 1045.6 %all-gather.4.cloned.1.call-start = ((), (), s32[]{:S(2)}) async-start(), calls=%async_computation.3 | async-start | bytes 14909440 | tf_op jit(solution)/shard_map/all_gather | solution.py:106
  13.4 661.8 %copy-start = (bf16[1,128,3584]{2,1,0:T(8,128)(2,1)S(1)}, bf16[1,128,3584]{2,1,0:T(8,128)(2,1)}, u32[]{:S(2)}) copy-start(bf16[1,128,3584]{2,1,0:T(8,128)(2,1)} %param.12) | copy-start | bytes 2752516
  679.1 383.2 %all-to-all-start.1 = ((bf16[128,4,256]{2,0,1:T(8,128)(2,1)}), bf16[128,4,256]{2,0,1:T(8,128)(2,1)S(1)}, u32[]{:S(2)}, u32[]{:S(2)}) async-start(bf16[128,4,256]{2,0,1:T(8,128)(2,1)} %pad_maximum_fusion.1), calls=%async_computation.1 | async-start | bytes 524288 | tf_op jit(solution)/shard_map/all_to_all | solution.py:119
  1062.3 56.9 %all-to-all-start = ((bf16[128,4,512]{0,2,1:T(8,128)(2,1)}), bf16[128,4,512]{0,2,1:T(8,128)(2,1)S(1)}, u32[]{:S(2)}, u32[]{:S(2)}) async-start(bf16[128,4,512]{0,2,1:T(8,128)(2,1)} %bitcast.10), calls=%async_computation | async-start | bytes 1048576 | tf_op jit(solution)/shard_map/all_to_all | solution.py:118
  1119.5 1.0 copy-start.1
Sparse Core Ops, SparseCore 0:
  9.1 313.7 all-gather.7
  324.7 350.3 all-gather.5
  676.9 376.6 all-gather.3
where the time goes:
time: 1160 us
  waiting for transfers between devices  1000 us (86%)
  starting transfers between devices  92.8 us (8%)
  matrix products  16.3 us (1%)
  blocking collectives  15 us (1%)
  local copies, waits for them, and re-layouts  14.1 us (1%)
  between operations  13.3 us (1%)
    all_gather x1, waiting for transfers between devices, body(): lax.all_gather(w_key, 'dp', axis=0, tiled=True)  349 us
    all_gather x1, waiting for transfers between devices, body(): lax.all_gather(w_query, 'dp', axis=0, tiled=True)  327 us
    all_gather x1, waiting for transfers between devices, body(): lax.all_gather(w_value, 'dp', axis=0, tiled=True)  310 us
    all_to_all x1, starting transfers between devices, body(): lax.all_to_all(pair_send, 'ctx', split_axis=1, concat_axis=0, tiled=True)  47.6 us
    all_to_all x1, starting transfers between devices, body(): lax.all_to_all(query_send, 'ctx', split_axis=1, concat_axis=0, tiled=True)  45.1 us
  transfers between devices with their start and end apart: 5, of which 4 were waited for; matrix products, arithmetic and copies ran while one was open for 2% of the time, Pallas kernels for 0%

commit v1 on v0

v1 whole, which is shorter than its diff:
```python
import functools

import jax
import jax.numpy as jnp
import numpy as np
from jax import lax
from jax.experimental import pallas as pl
from jax.experimental.pallas import tpu as pltpu
from jax.sharding import Mesh
from jax.sharding import PartitionSpec as P

KVH = 4
HEAD = 128
QHEADS = 16
BLOCK = 128
MAXB = 4
EPSILON = 1e-06
THETA = 1000000.0

AXES = ("y", "zl", "x", "zh", "core")
OFFSETS = (0, -1, 1, 2)
DOC = ("y", "zl", "x")
CTX = ("zh", "core")


def z_index(z):
    return (z % 4) * 2 + (z % 8) // 4


def plane_perm(first, shift):
    pairs = []
    for y in range(4):
        for x in range(4):
            for core in range(2):
                along_y = (core == 0) == first
                to_y = (y + shift) % 4 if along_y else y
                to_x = x if along_y else (x + shift) % 4
                pairs.append(((y * 4 + x) * 2 + core, (to_y * 4 + to_x) * 2 + core))
    return pairs


Z_PERMS = (
    [(z_index(z), z_index(z + 1)) for z in range(8)],
    [(z_index(z), z_index(z - 1)) for z in range(8)],
    [(z_index(z), z_index(z + 2 if z % 2 == 0 else z - 2)) for z in range(8)],
)


def send_three(block, axes, perms):
    return tuple(lax.ppermute(block, axes, perm) for perm in perms)


def attention_kernel(blocks_ref, counts_ref, qkv_ref, bias_ref, cos_ref, sin_ref, out_ref, q_scr, k_scr, v_scr):
    heads = q_scr.shape[0]
    cosine = cos_ref[...]
    sine = sin_ref[...]

    def rotated(column):
        value = qkv_ref[:, column : column + HEAD] + bias_ref[:, column : column + HEAD]
        return value * cosine + pltpu.roll(value, HEAD // 2, 1) * sine

    for head in range(heads):
        q_scr[head] = rotated(head * HEAD).astype(jnp.bfloat16)
    k_scr[...] = rotated(heads * HEAD).astype(jnp.bfloat16)
    start = (heads + 1) * HEAD
    v_scr[...] = (qkv_ref[:, start : start + HEAD] + bias_ref[:, start : start + HEAD]).astype(jnp.bfloat16)
    row = lax.broadcasted_iota(jnp.int32, (BLOCK, BLOCK), 0)
    column = lax.broadcasted_iota(jnp.int32, (BLOCK, BLOCK), 1)
    for head in range(heads):
        for block in range(4):
            query = q_scr[head, block * BLOCK : (block + 1) * BLOCK, :]
            count = counts_ref[head * 4 + block]
            total = jnp.zeros((BLOCK, 1), jnp.float32)
            mixed = jnp.zeros((BLOCK, HEAD), jnp.float32)
            for other in range(block + 1):
                keys = k_scr[other * BLOCK : (other + 1) * BLOCK, :]
                values = v_scr[other * BLOCK : (other + 1) * BLOCK, :]
                score = lax.dot_general(query, keys, (((1,), (1,)), ((), ())), preferred_element_type=jnp.float32)
                expo = jnp.exp(score * HEAD ** (-0.5))
                if other == block:
                    expo = jnp.where(column <= row, expo, 0.0)
                else:
                    seen = jnp.int32(0)
                    for slot in range(1, MAXB):
                        hit = (blocks_ref[(head * 4 + block) * MAXB + slot] == other) & (slot < count)
                        seen = seen | hit.astype(jnp.int32)
                    expo = jnp.where(seen > 0, expo, 0.0)
                total = total + jnp.sum(expo, axis=-1, keepdims=True)
                mixed = mixed + jnp.dot(expo.astype(jnp.bfloat16), values, preferred_element_type=jnp.float32)
            out_ref[block, :, head * HEAD : (head + 1) * HEAD] = (mixed / total).astype(jnp.bfloat16)


def attend(kv_blocks, block_counts, qkv, bias, cosine, sine):
    tokens = qkv.shape[0]
    heads = kv_blocks.shape[0]
    vmem = pl.BlockSpec(memory_space=pltpu.VMEM)
    smem = pl.BlockSpec(memory_space=pltpu.SMEM)
    return pl.pallas_call(
        attention_kernel,
        out_shape=jax.ShapeDtypeStruct((tokens // BLOCK, BLOCK, heads * HEAD), jnp.bfloat16),
        in_specs=[smem, smem, vmem, vmem, vmem, vmem],
        out_specs=vmem,
        scratch_shapes=[
            pltpu.VMEM((heads, tokens, HEAD), jnp.bfloat16),
            pltpu.VMEM((tokens, HEAD), jnp.bfloat16),
            pltpu.VMEM((tokens, HEAD), jnp.bfloat16),
        ],
        compiler_params=pltpu.CompilerParams(vmem_limit_bytes=32 * 1024 * 1024),
    )(kv_blocks.reshape(-1), block_counts.reshape(-1), qkv, bias, cosine, sine)


def rms_norm(tokens, norm_gain):
    floats = tokens.astype(jnp.float32)
    meansq = jnp.mean(floats * floats, axis=-1, keepdims=True)
    return (floats * lax.rsqrt(meansq + EPSILON) * norm_gain.astype(jnp.float32)).astype(jnp.bfloat16)


def rotary_tables(tokens):
    half = HEAD // 2
    exponent = jnp.arange(half, dtype=jnp.float32) * (2.0 / HEAD)
    inverse = jnp.power(jnp.float32(THETA), -exponent)
    angles = jnp.arange(tokens, dtype=jnp.float32)[:, None] * inverse[None, :]
    cosine = jnp.cos(angles)
    sine = jnp.sin(angles)
    return jnp.concatenate([cosine, cosine], axis=1), jnp.concatenate([-sine, sine], axis=1)


def body(hidden, norm_gain, w_query, w_key, w_value, bias_query, bias_key, bias_value, kv_blocks, block_counts):
    y, zl, x = (lax.axis_index(name) for name in DOC)
    zh, core = (lax.axis_index(name) for name in CTX)
    group = zh * 2 + core
    rows = w_query.shape[0]

    def own(weight, axis=1, group=group):
        width = weight.shape[axis] // 4
        return lax.dynamic_slice_in_dim(weight, group * width, width, axis)

    def columns_of(half):
        return jnp.concatenate([own(weight, 1, half * 2 + core) for weight in (w_query, w_key, w_value)], axis=1)

    bias = jnp.concatenate([own(bias_query, 0), own(bias_key, 0), own(bias_value, 0)])[None, :].astype(jnp.float32)

    z = zh * 4 + zl
    targets = (z + 1, z - 1, jnp.where(z % 2 == 0, z + 2, z - 2))
    shard = jnp.stack(
        [columns_of(zh)]
        + [
            lax.ppermute(columns_of((target % 8) // 4), ("zl", "zh"), perm)
            for target, perm in zip(targets, Z_PERMS, strict=True)
        ]
    )
    plane = ("y", "x", "core")
    first = [plane_perm(True, shift) for shift in (1, -1, 2)]
    second = [plane_perm(False, shift) for shift in (1, -1, 2)]
    shard = jnp.stack([shard, *send_three(shard, plane, first)])
    pieces = (shard, *send_three(shard, plane, second))

    normed = rms_norm(hidden[0], norm_gain)
    turned = normed.T.reshape(64, rows, BLOCK)
    offsets = jnp.array(OFFSETS, jnp.int32)
    ys, zs, xs = ((here + offsets) % 4 for here in (y, zl, x))
    index = (ys[:, None, None] * 4 + zs[None, None, :]) * 4 + xs[None, :, None]
    turned = turned[index.reshape(-1)].reshape(4, 4, 4 * rows, BLOCK)
    swap = lambda name, size: functools.partial(
        lax.ppermute, axis_name=name, perm=[(i, (i + 1) % size) for i in range(size)]
    )
    far = swap("zh", 2)(turned)
    near = swap("core", 2)(turned)
    far_near = swap("core", 2)(far)
    here_pair = jnp.stack([jnp.where(core == 0, turned, near), jnp.where(core == 0, near, turned)])
    far_pair = jnp.stack([jnp.where(core == 0, far, far_near), jnp.where(core == 0, far_near, far)])
    every = jnp.concatenate([jnp.where(zh == 0, here_pair, far_pair), jnp.where(zh == 0, far_pair, here_pair)])
    every = jnp.where(core == 0, every.transpose(0, 2, 1, 3, 4), every)
    summed = None
    for r, piece in enumerate(pieces):
        left = every[:, r].reshape(4, 4 * 4 * rows, BLOCK)
        part = lax.dot_general(
            left, piece.reshape(16 * rows, -1), (((1,), (0,)), ((), ())), preferred_element_type=jnp.float32
        )
        summed = part if summed is None else summed + part
    qkv = summed.reshape(4 * BLOCK, -1)
    cosine, sine = rotary_tables(4 * BLOCK)
    mixed = attend(kv_blocks, block_counts, qkv, bias, cosine, sine)
    back = lax.all_to_all(mixed, CTX, split_axis=0, concat_axis=0, tiled=True)
    return back.transpose(1, 0, 2).reshape(1, BLOCK, QHEADS * HEAD)


def solution(mesh):
    inner = Mesh(mesh.devices.reshape(4, 4, 4, 2, 2), AXES)
    rows = P(DOC, None)
    placed = (P(DOC, CTX, None), P(), rows, rows, rows, P(), P(), P(), P(CTX, None, None), P(CTX, None))
    return jax.shard_map(body, mesh=inner, in_specs=placed, out_specs=P(DOC, CTX, None), check_vma=False)
```

time: 1160 us -> 134 us (0.12)
  waiting for transfers between devices: 1000 us -> 54.7 us
  starting transfers between devices: 92.8 us -> 36.4 us
  between operations: 13.3 us -> 0.33 us
  matrix products: 16.3 us -> 4.29 us
    all_gather x3 -> x0, waiting for transfers between devices: 986 us -> none  [the longest x1 349 us: body(): lax.all_gather(w_key, 'dp', axis=0, tiled=True)]
    all_to_all x2 -> x0, starting transfers between devices: 92.7 us -> none  [the longest x1 47.6 us: body(): lax.all_to_all(pair_send, 'ctx', split_axis=1, concat_axis=0, tiled=True)]
    ppermute x0 -> x12, waiting for transfers between devices: none -> 54.7 us  [the longest x6 32 us: send_three(): return tuple((lax.ppermute(block, axes, perm) for perm in perms))]
    ppermute x0 -> x12, starting transfers between devices: none -> 36.4 us  [the longest x1 16 us: body(): far_near = swap('core', 2)(far)]
    dot_general x11 -> x4, matrix products: 16.3 us -> 4.29 us  [body(): lax.dot_general(left, piece.reshape(16 * rows, -1), (((1,), (0,)), ((), (...]
    all_to_all x2 -> x0, waiting for transfers between devices: 11.9 us -> none  [the longest x1 11.9 us: body(): lax.all_to_all(query_send, 'ctx', split_axis=1, concat_axis=0, tiled=True)]
  transfers between devices with their start and end apart: 5 -> 12, of which waited for: 4 -> 7; matrix products, arithmetic and copies ran while one was open for 2% -> 7% of each run, Pallas kernels for 0% -> 0%
where the time goes in v1:
time: 134 us
  waiting for transfers between devices  54.7 us (41%)
  starting transfers between devices  36.4 us (27%)
  blocking collectives  23.1 us (17%)
  other arithmetic  6.31 us (5%)
  local copies, waits for them, and re-layouts  5.15 us (4%)
  matrix products  4.29 us (3%)
  Pallas kernels  3.74 us (3%)
    ppermute x6, waiting for transfers between devices, send_three(): return tuple((lax.ppermute(block, axes, perm) for perm in perms))  32 us
    all_to_all x1, blocking collectives, body(): back = lax.all_to_all(mixed, CTX, split_axis=0, concat_axis=0, tiled=True)  23.1 us
    ppermute x1, waiting for transfers between devices, body(): far = swap('zh', 2)(turned)  19.7 us
    ppermute x1, starting transfers between devices, body(): far_near = swap('core', 2)(far)  16 us
    ppermute x6, starting transfers between devices, send_three(): return tuple((lax.ppermute(block, axes, perm) for perm in perms))  8.75 us
    ppermute x1, starting transfers between devices, body(): far = swap('zh', 2)(turned)  7.83 us
    dot_general x4, matrix products, body(): lax.dot_general(left, piece.reshape(16 * rows, -1), (((1,), (0,)), ((), (...  4.29 us
    pallas_call x1, Pallas kernels, attend(): pl.pallas_call(attention_kernel, out_shape=jax.ShapeDtypeStruct((tokens /...  3.74 us
  transfers between devices with their start and end apart: 12, of which 7 were waited for; matrix products, arithmetic and copies ran while one was open for 7% of the time, Pallas kernels for 0%

profile of v1, /device:TPU:1, one launch (start us, length us, event | category | flops | bytes accessed | tf_op | source)
XLA Modules:
  0.0 134.1 jit_solution(10058739595588773179)
XLA Ops:
  0.0 1.6 %copy.16 = bf16[1,128,3584]{1,2,0:T(8,128)(2,1)S(1)} copy(bf16[1,128,3584]{2,1,0:T(8,128)(2,1)} %param.11) | data formatting | bytes 1835008 | tf_op args[0]
  1.6 0.0 copy-done.3
  1.6 0.5 fusion
  2.1 0.0 copy-done.6
  2.1 0.1 add_multiply_fusion
  2.2 0.1 broadcast_add_fusion
  2.3 0.1 add.203
  2.4 0.0 copy-start.1
  2.4 0.0 copy-start.2
  2.4 0.5 fusion.2
  3.0 0.0 copy-start
  3.0 0.0 copy-start.7
  3.0 0.0 copy-start.8
  3.0 0.0 copy-start.4
  3.0 0.0 copy-start.5
  3.0 0.7 gather_fusion
  3.8 7.8 %collective-permute-start.1 = (bf16[4,4,224,128]{3,2,1,0:T(8,128)(2,1)S(1)}, bf16[4,4,224,128]{3,2,1,0:T(8,128)(2,1)}, u32[]{:S(2)}, u32[]{:S(2)}) collective-permute-start(bf16[4,4,224,128]{3,2,1,0:T(8,128)(2,1)S(1)} %bitcast.68), channel_id=1, source_target_pairs={{0,2},{2,0},{1,3},{3,1},{4,6},{6,4},{5,7},{7,5},{8,10},{10,8},{9,1... | collective-permute-start | bytes 2752520 | tf_op jit(solution)/shard_map/ppermute | solution.py:167
  11.6 1.0 collective-permute-start
  12.6 0.0 copy-done.2
  12.7 1.3 collective-permute-start.5
  14.0 0.1 collective-permute-start.4
  14.1 1.5 %collective-permute-start.3 = (bf16[56,768]{1,0:T(8,128)(2,1)S(1)}, bf16[56,768]{1,0:T(8,128)(2,1)S(1)}, u32[]{:S(2)}, u32[]{:S(2)}) collective-permute-start(bf16[56,768]{1,0:T(8,128)(2,1)S(1)} %pad_maximum_fusion.7), channel_id=1, source_target_pairs={{0,16},{16,32},{32,48},{48,2},{2,18},{18,34},{34,50},{50,0},{1,17}... | collective-permute-start | bytes 258056 | tf_op jit(solution)/shard_map/ppermute | solution.py:148
  15.6 0.8 dynamic_slice.57
  16.4 0.1 dynamic-slice_bitcast_fusion
  16.5 0.1 reshape.152.blocks_ref
  16.5 0.0 copy-done.5
  16.6 0.1 reshape.153.counts_ref
  16.7 19.7 %collective-permute-done.1 = bf16[4,4,224,128]{3,2,1,0:T(8,128)(2,1)} collective-permute-done((bf16[4,4,224,128]{3,2,1,0:T(8,128)(2,1)S(1)}, bf16[4,4,224,128]{3,2,1,0:T(8,128)(2,1)}, u32[]{:S(2)}, u32[]{:S(2)}) %collective-permute-start.1) | collective-permute-done | bytes 917536 | tf_op jit(solution)/shard_map/ppermute | solution.py:167
  36.4 16.0 %collective-permute-start.2 = (bf16[4,4,224,128]{3,2,1,0:T(8,128)(2,1)}, bf16[4,4,224,128]{3,2,1,0:T(8,128)(2,1)S(1)}, u32[]{:S(2)}, u32[]{:S(2)}) collective-permute-start(bf16[4,4,224,128]{3,2,1,0:T(8,128)(2,1)} %collective-permute-done.1), channel_id=1, source_target_pairs={{0,1},{1,0},{2,3},{3,2},{4,5},{5,4},{6,7},{7,6},{8,9},{9,8},{10,11... | collective-permute-start | bytes 2752520 | tf_op jit(solution)/shard_map/ppermute | solution.py:169
  52.4 0.3 collective-permute-done.5
  52.7 2.7 %collective-permute-done.4 = bf16[56,768]{1,0:T(8,128)(2,1)S(1)} collective-permute-done((bf16[56,768]{1,0:T(8,128)(2,1)S(1)}, bf16[56,768]{1,0:T(8,128)(2,1)S(1)}, u32[]{:S(2)}, u32[]{:S(2)}) %collective-permute-start.4) | collective-permute-done | bytes 86048 | tf_op jit(solution)/shard_map/ppermute | solution.py:148
  55.4 0.0 collective-permute-done.3
  55.4 0.1 fusion.11
  55.5 2.8 %collective-permute-start.8 = (bf16[4,56,768]{2,1,0:T(8,128)(2,1)S(1)}, bf16[4,56,768]{2,1,0:T(8,128)(2,1)S(1)}, u32[]{:S(2)}, u32[]{:S(2)}) collective-permute-start(bf16[4,56,768]{2,1,0:T(8,128)(2,1)S(1)} %get-tuple-element.16), channel_id=1, source_target_pairs={{0,128},{1,9},{4,132},{5,13},{8,136},{9,1},{12,140},{13,5},{64,192... | collective-permute-start | bytes 1032200 | tf_op jit(solution)/shard_map/ppermute | solution.py:50
  58.3 0.9 collective-permute-start.7
  59.1 0.6 collective-permute-start.6
  59.8 1.0 fusion.5
  60.7 0.2 pad_maximum_fusion.5
  61.0 2.5 %collective-permute-done.8 = bf16[4,56,768]{2,1,0:T(8,128)(2,1)S(1)} collective-permute-done((bf16[4,56,768]{2,1,0:T(8,128)(2,1)S(1)}, bf16[4,56,768]{2,1,0:T(8,128)(2,1)S(1)}, u32[]{:S(2)}, u32[]{:S(2)}) %collective-permute-start.8) | collective-permute-done | bytes 344096 | tf_op jit(solution)/shard_map/ppermute | solution.py:50
  63.4 3.8 %collective-permute-done.7 = bf16[4,56,768]{2,1,0:T(8,128)(2,1)S(1)} collective-permute-done((bf16[4,56,768]{2,1,0:T(8,128)(2,1)S(1)}, bf16[4,56,768]{2,1,0:T(8,128)(2,1)S(1)}, u32[]{:S(2)}, u32[]{:S(2)}) %collective-permute-start.7) | collective-permute-done | bytes 344096 | tf_op jit(solution)/shard_map/ppermute | solution.py:50
  67.3 0.0 collective-permute-done.6
  67.3 0.2 pad_maximum_fusion.3
  67.4 2.8 %collective-permute-start.10 = (bf16[4,4,56,768]{3,2,1,0:T(8,128)(2,1)S(1)}, bf16[4,4,56,768]{3,2,1,0:T(8,128)(2,1)S(1)}, u32[]{:S(2)}, u32[]{:S(2)}) collective-permute-start(bf16[4,4,56,768]{3,2,1,0:T(8,128)(2,1)S(1)} %pad_maximum_fusion.3), channel_id=1, source_target_pairs={{0,12},{1,193},{4,0},{5,197},{8,4},{9,201},{12,8},{13,205},{64,76}... | collective-permute-start | bytes 4128776 | tf_op jit(solution)/shard_map/ppermute | solution.py:50
  70.3 0.0 collective-permute-start.9
  70.3 1.6 %collective-permute-start.11 = (bf16[4,4,56,768]{3,2,1,0:T(8,128)(2,1)S(1)}, bf16[4,4,56,768]{3,2,1,0:T(8,128)(2,1)S(1)}, u32[]{:S(2)}, u32[]{:S(2)}) collective-permute-start(bf16[4,4,56,768]{3,2,1,0:T(8,128)(2,1)S(1)} %pad_maximum_fusion.3), channel_id=1, source_target_pairs={{0,8},{1,129},{4,12},{5,133},{8,0},{9,137},{12,4},{13,141},{64,72}... | collective-permute-start | bytes 4128776 | tf_op jit(solution)/shard_map/ppermute | solution.py:50
  71.9 0.0 collective-permute-done
  71.9 1.3 select_bitcast_fusion.3
  73.2 0.0 collective-permute-done.2
  73.2 1.3 select_bitcast_fusion.1
  74.5 0.4 broadcast_select_fusion.1
  74.9 0.3 pad_maximum_fusion
  75.3 0.3 bitcast_select_fusion
  75.6 0.3 fusion.12
  75.9 24.3 %collective-permute-done.10 = bf16[4,4,56,768]{3,2,1,0:T(8,128)(2,1)S(1)} collective-permute-done((bf16[4,4,56,768]{3,2,1,0:T(8,128)(2,1)S(1)}, bf16[4,4,56,768]{3,2,1,0:T(8,128)(2,1)S(1)}, u32[]{:S(2)}, u32[]{:S(2)}) %collective-permute-start.10) | collective-permute-done | bytes 1376288 | tf_op jit(solution)/shard_map/ppermute | solution.py:50
  100.3 1.0 fusion.15
  101.3 1.0 fusion.13
  102.3 1.3 collective-permute-done.9
  103.7 1.0 fusion.14
  104.7 0.0 collective-permute-done.11
  104.7 1.2 add_add_fusion
  105.9 3.7 %shard_map.109 = bf16[4,128,512]{2,1,0:T(8,128)(2,1)S(1)} custom-call(s32[64]{0:T(128)S(1)} %reshape.152.blocks_ref, s32[16]{0:T(128)S(1)} %reshape.153.counts_ref, f32[512,768]{1,0:T(8,128)S(1)} %bitcast.61, f32[1,768]{1,0:T(1,128)S(1)} %maximum_convert_fusion.bias_ref, f32[512,128]{1,0:T(8,128)S(1)} %get-tuple-element.41.cos_ref, ...), custom_call_target="tpu_custom_call" | custom-call | tf_op jit(solution)/shard_map/pallas_call | solution.py:98
  109.6 23.1 %all_to_all.5 = bf16[4,128,512]{2,1,0:T(8,128)(2,1)S(1)} all-to-all(bf16[4,128,512]{2,1,0:T(8,128)(2,1)S(1)} %shard_map.109), channel_id=1, replica_groups=mesh['y'=4,'zl'=4,'x'=4,'zh'=2,'core'=2] {'zh','core'}, dimensions={0} | all-to-all | bytes 1048576 | tf_op jit(solution)/shard_map/all_to_all | solution.py:184
  132.8 0.3 copy.22
  133.0 1.0 copy.23
  (21 shorter events, 0.2 us)
Async XLA Ops:
  0.0 2.1 %copy-start.6 = (s32[4]{0:T(128)S(1)}, s32[4]{0:T(128)}, u32[]{:S(2)}) copy-start(s32[4]{0:T(128)} %constant.128.clone) | copy-start | bytes 52
  0.0 1.6 %copy-start.3 = (bf16[3584]{0:T(1024)(128)(2,1)S(1)}, bf16[3584]{0:T(1024)(128)(2,1)}, u32[]{:S(2)}) copy-start(bf16[3584]{0:T(1024)(128)(2,1)} %param.12) | copy-start | bytes 21508
  2.4 10.2 %copy-start.1 = (bf16[56,512]{1,0:T(8,128)(2,1)S(1)}, bf16[56,512]{1,0:T(8,128)(2,1)}, u32[]{:S(2)}) copy-start(bf16[56,512]{1,0:T(8,128)(2,1)} %param.15) | copy-start | bytes 172036
  2.4 10.1 %copy-start.2 = (bf16[56,512]{1,0:T(8,128)(2,1)S(1)}, bf16[56,512]{1,0:T(8,128)(2,1)}, u32[]{:S(2)}) copy-start(bf16[56,512]{1,0:T(8,128)(2,1)} %param.14) | copy-start | bytes 172036
  3.0 9.6 %copy-start = (bf16[56,2048]{1,0:T(8,128)(2,1)S(1)}, bf16[56,2048]{1,0:T(8,128)(2,1)}, u32[]{:S(2)}) copy-start(bf16[56,2048]{1,0:T(8,128)(2,1)} %param.13) | copy-start | bytes 688132
  3.0 13.4 %copy-start.7 = (bf16[512]{0:T(512)(128)(2,1)S(1)}, bf16[512]{0:T(512)(128)(2,1)}, u32[]{:S(2)}) copy-start(bf16[512]{0:T(512)(128)(2,1)} %param.18) | copy-start | bytes 3076
  3.0 13.4 %copy-start.8 = (bf16[512]{0:T(512)(128)(2,1)S(1)}, bf16[512]{0:T(512)(128)(2,1)}, u32[]{:S(2)}) copy-start(bf16[512]{0:T(512)(128)(2,1)} %param.17) | copy-start | bytes 3076
  3.0 13.4 %copy-start.4 = (s32[4,4,4]{2,1,0:T(4,128)S(1)}, s32[4,4,4]{2,1,0:T(4,128)}, u32[]{:S(2)}) copy-start(s32[4,4,4]{2,1,0:T(4,128)} %param.19) | copy-start | bytes 772
  3.0 13.5 %copy-start.5 = (s32[4,4]{1,0:T(4,128)S(1)}, s32[4,4]{1,0:T(4,128)}, u32[]{:S(2)}) copy-start(s32[4,4]{1,0:T(4,128)} %param.20) | copy-start | bytes 196
  3.8 32.6 %collective-permute-start.1 = (bf16[4,4,224,128]{3,2,1,0:T(8,128)(2,1)S(1)}, bf16[4,4,224,128]{3,2,1,0:T(8,128)(2,1)}, u32[]{:S(2)}, u32[]{:S(2)}) collective-permute-start(bf16[4,4,224,128]{3,2,1,0:T(8,128)(2,1)S(1)} %bitcast.68), channel_id=1, source_target_pairs={{0,2},{2,0},{1,3},{3,1},{4,6},{6,4},{5,7},{7,5},{8,10},{10,8},{9,1... | collective-permute-start | bytes 2752520 | tf_op jit(solution)/shard_map/ppermute | solution.py:167
  11.6 60.3 %collective-permute-start = (bf16[4,4,224,128]{3,2,1,0:T(8,128)(2,1)S(1)}, bf16[4,4,224,128]{3,2,1,0:T(8,128)(2,1)}, u32[]{:S(2)}, u32[]{:S(2)}) collective-permute-start(bf16[4,4,224,128]{3,2,1,0:T(8,128)(2,1)S(1)} %bitcast.69), channel_id=1, source_target_pairs={{0,1},{1,0},{2,3},{3,2},{4,5},{5,4},{6,7},{7,6},{8,9},{9,8},{10,11... | collective-permute-start | bytes 2752520 | tf_op jit(solution)/shard_map/ppermute | solution.py:168
  12.7 40.0 %collective-permute-start.5 = (bf16[56,768]{1,0:T(8,128)(2,1)S(1)}, bf16[56,768]{1,0:T(8,128)(2,1)S(1)}, u32[]{:S(2)}, u32[]{:S(2)}) collective-permute-start(bf16[56,768]{1,0:T(8,128)(2,1)S(1)} %pad_maximum_fusion.9), channel_id=1, source_target_pairs={{0,32},{16,50},{32,2},{48,16},{2,34},{18,48},{34,0},{50,18},{1,33}... | collective-permute-start | bytes 258056 | tf_op jit(solution)/shard_map/ppermute | solution.py:148
  14.0 41.4 %collective-permute-start.4 = (bf16[56,768]{1,0:T(8,128)(2,1)S(1)}, bf16[56,768]{1,0:T(8,128)(2,1)S(1)}, u32[]{:S(2)}, u32[]{:S(2)}) collective-permute-start(bf16[56,768]{1,0:T(8,128)(2,1)S(1)} %pad_maximum_fusion.8), channel_id=1, source_target_pairs={{0,50},{16,0},{32,16},{48,32},{2,48},{18,2},{34,18},{50,34},{1,51}... | collective-permute-start | bytes 258056 | tf_op jit(solution)/shard_map/ppermute | solution.py:148
  14.1 41.3 %collective-permute-start.3 = (bf16[56,768]{1,0:T(8,128)(2,1)S(1)}, bf16[56,768]{1,0:T(8,128)(2,1)S(1)}, u32[]{:S(2)}, u32[]{:S(2)}) collective-permute-start(bf16[56,768]{1,0:T(8,128)(2,1)S(1)} %pad_maximum_fusion.7), channel_id=1, source_target_pairs={{0,16},{16,32},{32,48},{48,2},{2,18},{18,34},{34,50},{50,0},{1,17}... | collective-permute-start | bytes 258056 | tf_op jit(solution)/shard_map/ppermute | solution.py:148
  36.4 36.8 %collective-permute-start.2 = (bf16[4,4,224,128]{3,2,1,0:T(8,128)(2,1)}, bf16[4,4,224,128]{3,2,1,0:T(8,128)(2,1)S(1)}, u32[]{:S(2)}, u32[]{:S(2)}) collective-permute-start(bf16[4,4,224,128]{3,2,1,0:T(8,128)(2,1)} %collective-permute-done.1), channel_id=1, source_target_pairs={{0,1},{1,0},{2,3},{3,2},{4,5},{5,4},{6,7},{7,6},{8,9},{9,8},{10,11... | collective-permute-start | bytes 2752520 | tf_op jit(solution)/shard_map/ppermute | solution.py:169
  55.5 8.0 %collective-permute-start.8 = (bf16[4,56,768]{2,1,0:T(8,128)(2,1)S(1)}, bf16[4,56,768]{2,1,0:T(8,128)(2,1)S(1)}, u32[]{:S(2)}, u32[]{:S(2)}) collective-permute-start(bf16[4,56,768]{2,1,0:T(8,128)(2,1)S(1)} %get-tuple-element.16), channel_id=1, source_target_pairs={{0,128},{1,9},{4,132},{5,13},{8,136},{9,1},{12,140},{13,5},{64,192... | collective-permute-start | bytes 1032200 | tf_op jit(solution)/shard_map/ppermute | solution.py:50
  58.3 9.0 %collective-permute-start.7 = (bf16[4,56,768]{2,1,0:T(8,128)(2,1)S(1)}, bf16[4,56,768]{2,1,0:T(8,128)(2,1)S(1)}, u32[]{:S(2)}, u32[]{:S(2)}) collective-permute-start(bf16[4,56,768]{2,1,0:T(8,128)(2,1)S(1)} %get-tuple-element.16), channel_id=1, source_target_pairs={{0,192},{1,13},{4,196},{5,1},{8,200},{9,5},{12,204},{13,9},{64,0},... | collective-permute-start | bytes 1032200 | tf_op jit(solution)/shard_map/ppermute | solution.py:50
  59.1 8.1 %collective-permute-start.6 = (bf16[4,56,768]{2,1,0:T(8,128)(2,1)S(1)}, bf16[4,56,768]{2,1,0:T(8,128)(2,1)S(1)}, u32[]{:S(2)}, u32[]{:S(2)}) collective-permute-start(bf16[4,56,768]{2,1,0:T(8,128)(2,1)S(1)} %get-tuple-element.16), channel_id=1, source_target_pairs={{0,64},{1,5},{4,68},{5,9},{8,72},{9,13},{12,76},{13,1},{64,128},{6... | collective-permute-start | bytes 1032200 | tf_op jit(solution)/shard_map/ppermute | solution.py:50
  67.4 32.8 %collective-permute-start.10 = (bf16[4,4,56,768]{3,2,1,0:T(8,128)(2,1)S(1)}, bf16[4,4,56,768]{3,2,1,0:T(8,128)(2,1)S(1)}, u32[]{:S(2)}, u32[]{:S(2)}) collective-permute-start(bf16[4,4,56,768]{3,2,1,0:T(8,128)(2,1)S(1)} %pad_maximum_fusion.3), channel_id=1, source_target_pairs={{0,12},{1,193},{4,0},{5,197},{8,4},{9,201},{12,8},{13,205},{64,76}... | collective-permute-start | bytes 4128776 | tf_op jit(solution)/shard_map/ppermute | solution.py:50
  70.3 33.4 %collective-permute-start.9 = (bf16[4,4,56,768]{3,2,1,0:T(8,128)(2,1)S(1)}, bf16[4,4,56,768]{3,2,1,0:T(8,128)(2,1)S(1)}, u32[]{:S(2)}, u32[]{:S(2)}) collective-permute-start(bf16[4,4,56,768]{3,2,1,0:T(8,128)(2,1)S(1)} %pad_maximum_fusion.3), channel_id=1, source_target_pairs={{0,4},{1,65},{4,8},{5,69},{8,12},{9,73},{12,0},{13,77},{64,68},{65... | collective-permute-start | bytes 4128776 | tf_op jit(solution)/shard_map/ppermute | solution.py:50
  70.3 34.4 %collective-permute-start.11 = (bf16[4,4,56,768]{3,2,1,0:T(8,128)(2,1)S(1)}, bf16[4,4,56,768]{3,2,1,0:T(8,128)(2,1)S(1)}, u32[]{:S(2)}, u32[]{:S(2)}) collective-permute-start(bf16[4,4,56,768]{3,2,1,0:T(8,128)(2,1)S(1)} %pad_maximum_fusion.3), channel_id=1, source_target_pairs={{0,8},{1,129},{4,12},{5,133},{8,0},{9,137},{12,4},{13,141},{64,72}... | collective-permute-start | bytes 4128776 | tf_op jit(solution)/shard_map/ppermute | solution.py:50
